TPU v7x, 32 devices: a whole 2x2x4 slice. The times are simulated.
32 devices in a mesh: events: 2 (over y), blk: 4 (over z), sub: 2 (over x), pair: 2 (over core).
Axes of the slice: x: 2, y: 2, z: 4, core: 2. Of those that a mesh axis runs over, the one named last changes fastest.
Arguments:
- synthetic: bfloat16 [2560, 4096], P(('events', 'sub', 'pair'), 'blk'), parts along dimension 0, may hold values from -6 to 6
- observed: bfloat16 [2560, 4096], P(('events', 'sub', 'pair'), 'blk'), parts along dimension 0, may hold values from -6 to 6
- station_weights: int32 [2560], P('events'), parts along dimension 0, may hold values from 1 to 4
- pair_mask: int32 [32, 16], P('events'), parts along dimension 0, may hold values from 0 to 1, as said below
Outputs:
- adjoint_traces: bfloat16 [2560, 4096], P(('events', 'sub', 'pair'), 'blk'), parts along dimension 0
There are 2 independent parts, one for each index of `events`. A program takes and returns all parts, laid end to end along the dimension named above; each array names one. Nothing has to cross between parts.
Inputs may be any that keep to these rules, and one draw needn't show every extreme that they name: pair_mask[p, q] is 1 where station pieces p and q are coupled; piece p holds stations p * 80 to (p + 1) * 80 - 1.
All inputs are finite; a program needn't handle non-finite values.
Results may differ from a plain program's by a relative error of at most 0.025.
Values may be sent and summed in bfloat16 or wider, within the bound.
A program may use at most 64 MiB of HBM per device.

v0:
```python
import math

import jax
import jax.numpy as jnp
from jax import lax
from jax.sharding import PartitionSpec as P

NT = 4096
NF = 512
F_LO = 64


epsilon = 1e-06


def from_behind(value, axis, steps):
    count = lax.axis_size(axis)
    pairs = [(source, (source + steps) % count) for source in range(count)]
    return lax.ppermute(value, axis, pairs)


def make_basis(first_sample, sample_count):
    sample_index = first_sample + jnp.arange(sample_count, dtype=jnp.int32)
    bin_index = F_LO + jnp.arange(NF, dtype=jnp.int32)
    phases = sample_index[:, None] * bin_index[None, :] % NT
    angles = phases.astype(jnp.float32) * (2.0 * math.pi / NT)
    return jnp.concatenate([jnp.cos(angles), -jnp.sin(angles)], axis=1).astype(jnp.bfloat16)


def spectral_rate(spectrum):
    angular = 2.0 * math.pi / NT * (F_LO + jnp.arange(NF, dtype=jnp.int32)).astype(jnp.float32)
    widened = spectrum.astype(jnp.float32)
    return jnp.concatenate([-angular * widened[:, NF:], angular * widened[:, :NF]], axis=1).astype(
        jnp.bfloat16
    )


def shards(synthetic, observed, station_weights, pair_mask):
    cycle_size = lax.axis_size("blk")
    groups = lax.axis_size("sub") * lax.axis_size("pair")
    block_index = lax.axis_index("blk")
    member = lax.axis_index("sub") * lax.axis_size("pair") + lax.axis_index("pair")
    time_span = synthetic.shape[1]
    piece_rows = synthetic.shape[0] // cycle_size
    stations = station_weights.shape[0]
    scale_factor = 1.0 / math.sqrt(NT)
    inverse_scale = 1.0 / math.sqrt(NF)
    contract_last = (((1,), (1,)), ((), ()))
    basis_rows = make_basis(block_index * time_span, time_span)
    summed = lax.psum_scatter(
        jnp.concatenate(
            [
                jnp.dot(synthetic, basis_rows, preferred_element_type=jnp.float32),
                jnp.dot(observed, basis_rows, preferred_element_type=jnp.float32),
            ],
            axis=1,
        ).astype(jnp.bfloat16),
        "blk",
        scatter_dimension=0,
        tiled=True,
    ).astype(jnp.float32)
    model_spec = (summed[:, : 2 * NF] * scale_factor).astype(jnp.bfloat16)
    data_spec = (summed[:, 2 * NF :] * scale_factor).astype(jnp.bfloat16)
    own_rates = jnp.concatenate([spectral_rate(model_spec), spectral_rate(data_spec)], axis=1)
    block_model, block_data = (
        lax.all_gather(model_spec, ("sub", "pair"), axis=0, tiled=True),
        lax.all_gather(data_spec, ("sub", "pair"), axis=0, tiled=True),
    )
    block_power = jnp.sum(jnp.square(spectral_rate(block_model).astype(jnp.float32)), axis=1)
    gains = station_weights.astype(jnp.float32).reshape(groups * cycle_size, piece_rows)
    block_gain = lax.dynamic_slice_in_dim(
        gains.reshape(groups, cycle_size, piece_rows), block_index, 1, 1
    ).reshape(groups * piece_rows)
    link_piece = jnp.maximum(pair_mask, pair_mask.T)
    block_link = lax.dynamic_slice_in_dim(
        link_piece.reshape(groups, cycle_size, groups * cycle_size), block_index, 1, 1
    ).reshape(groups, groups * cycle_size)
    factor = 4.0 / math.sqrt(stations)

    def pair_tile(running, carried, source):
        column_model = carried[:, : 2 * NF]
        column_data = carried[:, 2 * NF :]
        column_piece = member * cycle_size + source
        column_gain = lax.dynamic_slice_in_dim(gains, column_piece, 1, 0)[0]
        column_power = jnp.sum(jnp.square(column_model.astype(jnp.float32)), axis=1)
        active_flags = lax.dynamic_slice_in_dim(block_link, column_piece, 1, 1)[:, 0]
        link_rows = jnp.broadcast_to(
            active_flags.astype(jnp.float32)[:, None], (groups, piece_rows)
        ).reshape(groups * piece_rows)
        cross_model = lax.dot_general(
            block_model, column_model, contract_last, preferred_element_type=jnp.float32
        )
        cross_data = lax.dot_general(
            block_data, column_data, contract_last, preferred_element_type=jnp.float32
        )
        normalizer = 0.5 * (block_power[:, None] + column_power[None, :]) + epsilon
        coupling = (
            factor
            * block_gain[:, None]
            * column_gain[None, :]
            * link_rows[:, None]
            * (cross_model - cross_data)
            / normalizer
        ).astype(jnp.bfloat16)
        return running + jnp.dot(coupling, column_model, preferred_element_type=jnp.float32)

    running = jnp.zeros((groups * piece_rows, 2 * NF), jnp.float32)
    running = pair_tile(running, own_rates, block_index)

    def cycle_turn(turn_index, loop_state):
        current, ahead_rates, behind_rates = loop_state
        ahead_rates = from_behind(ahead_rates, "blk", 1)
        behind_rates = from_behind(behind_rates, "blk", -1)
        current = pair_tile(current, ahead_rates, (block_index - turn_index) % cycle_size)
        current = pair_tile(current, behind_rates, (block_index + turn_index) % cycle_size)
        return (current, ahead_rates, behind_rates)

    running, ahead_rates, behind_rates = lax.fori_loop(
        1, cycle_size // 2, cycle_turn, (running, own_rates, own_rates)
    )
    ahead_rates = from_behind(ahead_rates, "blk", 1)
    running = pair_tile(running, ahead_rates, (block_index - cycle_size // 2) % cycle_size)
    adjoint_spec = lax.psum_scatter(
        running.astype(jnp.bfloat16), ("sub", "pair"), scatter_dimension=0, tiled=True
    )
    return (
        lax.dot_general(
            lax.all_gather(adjoint_spec, "blk", axis=0, tiled=True),
            basis_rows,
            contract_last,
            preferred_element_type=jnp.float32,
        )
        * inverse_scale
    ).astype(jnp.bfloat16)


def solution(mesh):
    placed = (
        P(("events", "sub", "pair"), "blk"),
        P(("events", "sub", "pair"), "blk"),
        P("events"),
        P("events", None),
    )
    return jax.shard_map(
        shards,
        mesh=mesh,
        in_specs=placed,
        out_specs=P(("events", "sub", "pair"), "blk"),
        check_vma=False,
    )
```

profile of v0, /device:TPU:0, one launch (start us, length us, event | category | flops | bytes accessed | tf_op | source)
XLA Modules:
  0.0 146.9 jit_solution(12198449554490275419)
XLA Ops:
  6.5 9.1 %cosine_convert_fusion = (bf16[1024,512]{1,0:T(8,128)(2,1)S(1)}, bf16[1024,512]{1,0:T(8,128)(2,1)S(1)}) fusion(s32[512]{0:T(512)S(1)} %iota_add_fusion.1, s32[1024]{0:T(1024)S(1)} %iota_add_fusion), kind=kLoop, calls=%fused_computation.10 | loop fusion | flops 8912896 | bytes 2103296 | tf_op jit(solution)/shard_map/convert.10
  15.7 0.9 fusion.6
  17.3 0.8 fusion.5
  18.1 1.2 pad_maximum_fusion.1
  22.1 31.5 %reduce-scatter.3.cloned.1.call-done = bf16[80,2048]{1,0:T(8,128)(2,1)} async-done(((bf16[320,2048]{1,0:T(8,128)(2,1)}), bf16[80,2048]{1,0:T(8,128)(2,1)}) %reduce-scatter.3.cloned.1.call-update) | async-done | bytes 327696 | tf_op jit(solution)/shard_map/reduce_scatter | solution.py:50
  53.6 1.0 convert_element_type.134
  54.8 7.9 %all_gather.9 = bf16[320,1024]{1,0:T(8,128)(2,1)S(1)} all-gather(bf16[80,1024]{1,0:T(8,128)(2,1)S(1)} %get-tuple-element.36), channel_id=1, replica_groups=mesh['events'=2,'blk'=4,'sub'=2,'pair'=2] {'sub','pair'}, dimensions={0}, use_global_device_ids=true | all-gather | bytes 819200 | tf_op jit(solution)/shard_map/all_gather | solution.py:66
  62.9 1.0 fusion.94
  63.8 0.7 pad_maximum_fusion.5
  64.6 3.8 %collective-permute-start.1 = (bf16[80,2048]{1,0:T(8,128)(2,1)}, bf16[80,2048]{1,0:T(8,128)(2,1)}, u32[]{:S(2)}, u32[]{:S(2)}) collective-permute-start(bf16[80,2048]{1,0:T(8,128)(2,1)} %pad_maximum_fusion.5), channel_id=1, source_target_pairs={{0,12},{4,0},{8,4},{12,8},{1,13},{5,1},{9,5},{13,9},{2,14},{6,2},{... | collective-permute-start | bytes 983048 | tf_op jit(solution)/shard_map/while/body/eval_jaxpr/ppermute | solution.py:19
  68.6 7.4 %all_gather.10 = bf16[320,1024]{1,0:T(8,128)(2,1)S(1)} all-gather(bf16[80,1024]{1,0:T(8,128)(2,1)S(1)} %get-tuple-element.30), channel_id=1, replica_groups=mesh['events'=2,'blk'=4,'sub'=2,'pair'=2] {'sub','pair'}, dimensions={0}, use_global_device_ids=true | all-gather | bytes 819200 | tf_op jit(solution)/shard_map/all_gather | solution.py:67
  76.9 1.8 %fusion.19 = f32[320,1024]{1,0:T(8,128)S(1)} fusion(f32[320,80]{1,0:T(8,128)} %fusion.94, bf16[320,1024]{1,0:T(8,128)(2,1)S(1)} %all_gather.10, bf16[80,512]{1,0:T(8,128)(2,1)S(1)} %get-tuple-element.66, bf16[80,512]{1,0:T(8,128)(2,1)} %copy-done.4, f32[80]{0:T(128)} %multiply_reduce_fusion.4, f32[320]{0:T(512)S(1)} %multiply_reduce_fusion, ...), kind=kOutput, calls=%fused_computation.39 | convolution fusion | flops 105743360 | bytes 2400640 | tf_op jit(solution)/shard_map/dot_general | solution.py:105
  78.9 1.1 multiply_reduce_fusion.3
  79.9 1.2 fusion.28
  81.9 1.9 %fusion.26 = f32[320,80]{1,0:T(8,128)} fusion(bf16[320,1024]{1,0:T(8,128)(2,1)S(1)} %all_gather.10, bf16[80,2048]{1,0:T(8,128)(2,1)} %collective-permute-done.1), kind=kOutput, calls=%fused_computation.55 | convolution fusion | flops 52428800 | bytes 921600 | tf_op jit(solution)/shard_map/while/body/eval_jaxpr/dot_general | solution.py:93
  83.8 2.9 %convolution_add_fusion.2 = f32[320,1024]{1,0:T(8,128)} fusion(f32[320,1024]{1,0:T(8,128)S(1)} %fusion.19, f32[320,80]{1,0:T(8,128)S(1)} %fusion.28, bf16[320,1024]{1,0:T(8,128)(2,1)S(1)} %all_gather.9, bf16[80,2048]{1,0:T(8,128)(2,1)} %collective-permute-done, f32[80]{0:T(128)S(1)} %multiply_reduce_fusion.3, f32[320]{0:T(512)S(1)} %mul.305, ...), kind=kOutput, calls=%fused_computation.14 | convolution fusion | flops 105415680 | bytes 3711360 | tf_op jit(solution)/shard_map/while/body/eval_jaxpr/dot_general | solution.py:105
  86.7 1.0 multiply_reduce_fusion.2
  87.8 2.4 %convolution_add_fusion.1 = f32[320,1024]{1,0:T(8,128)S(1)} fusion(f32[320,1024]{1,0:T(8,128)} %convolution_add_fusion.2, f32[320,80]{1,0:T(8,128)} %fusion.26, bf16[320,1024]{1,0:T(8,128)(2,1)S(1)} %all_gather.9, bf16[80,2048]{1,0:T(8,128)(2,1)} %collective-permute-done.1, f32[80]{0:T(128)S(1)} %multiply_reduce_fusion.2, f32[320]{0:T(512)S(1)} %mul.313, ...), kind=kOutput, calls=%fused_computation.13 | convolution fusion | flops 105415680 | bytes 3711360 | tf_op jit(solution)/shard_map/while/body/eval_jaxpr/dot_general | solution.py:105
  90.9 1.2 fusion.24
  92.2 1.0 multiply_reduce_fusion.1
  93.2 2.7 %fusion.3 = bf16[320,1024]{1,0:T(8,128)(2,1)} fusion(f32[320,1024]{1,0:T(8,128)S(1)} %convolution_add_fusion.1, f32[320,80]{1,0:T(8,128)S(1)} %fusion.24, bf16[320,1024]{1,0:T(8,128)(2,1)S(1)} %all_gather.9, bf16[80,2048]{1,0:T(8,128)(2,1)} %collective-permute-done.2, f32[80]{0:T(128)S(1)} %multiply_reduce_fusion.1, f32[320]{0:T(512)S(1)} %mul.321, ...), kind=kOutput, calls=%fused_computation.15 | convolution fusion | flops 105743360 | bytes 3056000 | tf_op jit(solution)/shard_map/dot_general | solution.py:105
  95.9 23.2 %reduce-scatter.5.cloned.1.call-done = bf16[80,1024]{1,0:T(8,128)(2,1)} async-done(((bf16[320,1024]{1,0:T(8,128)(2,1)}), bf16[80,1024]{1,0:T(8,128)(2,1)}) %reduce-scatter.5.cloned.1.call-update) | async-done | bytes 163856 | tf_op jit(solution)/shard_map/reduce_scatter | solution.py:123
  119.1 18.0 %all_gather.11 = bf16[320,1024]{1,0:T(8,128)(2,1)S(1)} all-gather(bf16[80,1024]{1,0:T(8,128)(2,1)} %reduce-scatter.5.cloned.1.call-done), channel_id=1, replica_groups=mesh['events'=2,'blk'=4,'sub'=2,'pair'=2] {'blk'}, dimensions={0}, use_global_device_ids=true | all-gather | bytes 819200 | tf_op jit(solution)/shard_map/all_gather | solution.py:128
  137.1 3.0 %fusion.4 = bf16[320,1024]{1,0:T(8,128)(2,1)} fusion(bf16[320,1024]{1,0:T(8,128)(2,1)S(1)} %all_gather.11, bf16[1024,512]{1,0:T(8,128)(2,1)} %copy-done.3, bf16[1024,512]{1,0:T(8,128)(2,1)S(1)} %copy-done.2), kind=kOutput, calls=%fused_computation.16 | convolution fusion | flops 675938304 | bytes 3407872 | tf_op jit(solution)/shard_map/dot_general | solution.py:127
  (61 shorter events, 6.3 us)
Async XLA Ops:
  6.5 9.2 %copy-start = (bf16[320,1024]{1,0:T(8,128)(2,1)S(1)}, bf16[320,1024]{1,0:T(8,128)(2,1)}, u32[]{:S(2)}) copy-start(bf16[320,1024]{1,0:T(8,128)(2,1)} %param.5) | copy-start | bytes 1966084
  6.5 47.1 %reduce-scatter.3.cloned.1.call-start = ((), (), s32[]{:S(2)}) async-start(), calls=%async_computation.2 | async-start | bytes 1638400 | tf_op jit(solution)/shard_map/reduce_scatter | solution.py:50
  15.7 1.0 copy-start.1
  15.7 1.4 copy-start.3
  15.7 1.6 %copy-start.8 = (bf16[320,1024]{1,0:T(8,128)(2,1)S(1)}, bf16[320,1024]{1,0:T(8,128)(2,1)}, u32[]{:S(2)}) copy-start(bf16[320,1024]{1,0:T(8,128)(2,1)} %param.4) | copy-start | bytes 1966084
  19.3 0.7 copy-start.6
  19.3 0.9 copy-start.5
  19.4 99.8 %reduce-scatter.5.cloned.1.call-start = ((), (), s32[]{:S(2)}) async-start(), calls=%async_computation.3 | async-start | bytes 819200 | tf_op jit(solution)/shard_map/reduce_scatter | solution.py:123
  62.9 1.7 %copy-start.4 = (bf16[80,512]{1,0:T(8,128)(2,1)}, bf16[80,512]{1,0:T(8,128)(2,1)S(1)}, u32[]{:S(2)}) copy-start(bf16[80,512]{1,0:T(8,128)(2,1)S(1)} %get-tuple-element.67) | copy-start | bytes 245764
  64.6 14.2 %collective-permute-start = (bf16[80,2048]{1,0:T(8,128)(2,1)}, bf16[80,2048]{1,0:T(8,128)(2,1)}, u32[]{:S(2)}, u32[]{:S(2)}) collective-permute-start(bf16[80,2048]{1,0:T(8,128)(2,1)} %pad_maximum_fusion.5), channel_id=1, source_target_pairs={{0,4},{4,8},{8,12},{12,0},{1,5},{5,9},{9,13},{13,1},{2,6},{6,10},{... | collective-permute-start | bytes 983048 | tf_op jit(solution)/shard_map/while/body/eval_jaxpr/ppermute | solution.py:19
  64.6 17.3 %collective-permute-start.1 = (bf16[80,2048]{1,0:T(8,128)(2,1)}, bf16[80,2048]{1,0:T(8,128)(2,1)}, u32[]{:S(2)}, u32[]{:S(2)}) collective-permute-start(bf16[80,2048]{1,0:T(8,128)(2,1)} %pad_maximum_fusion.5), channel_id=1, source_target_pairs={{0,12},{4,0},{8,4},{12,8},{1,13},{5,1},{9,5},{13,9},{2,14},{6,2},{... | collective-permute-start | bytes 983048 | tf_op jit(solution)/shard_map/while/body/eval_jaxpr/ppermute | solution.py:19
  78.8 5.0 %copy-start.7 = (f32[80]{0:T(128)S(1)}, f32[80]{0:T(128)}, u32[]{:S(2)}) copy-start(f32[80]{0:T(128)} %get-tuple-element.58) | copy-start | bytes 964
  78.8 12.1 %collective-permute-start.2 = (bf16[80,2048]{1,0:T(8,128)(2,1)}, bf16[80,2048]{1,0:T(8,128)(2,1)}, u32[]{:S(2)}, u32[]{:S(2)}) collective-permute-start(bf16[80,2048]{1,0:T(8,128)(2,1)} %collective-permute-done), channel_id=1, source_target_pairs={{0,4},{4,8},{8,12},{12,0},{1,5},{5,9},{9,13},{13,1},{2,6},{6,10},{... | collective-permute-start | bytes 983048 | tf_op jit(solution)/shard_map/ppermute | solution.py:19
  95.9 41.2 %copy-start.2 = (bf16[1024,512]{1,0:T(8,128)(2,1)S(1)}, bf16[1024,512]{1,0:T(8,128)(2,1)}, u32[]{:S(2)}) copy-start(bf16[1024,512]{1,0:T(8,128)(2,1)} %copy-done.1) | copy-start | bytes 3145732
Sparse Core Ops, SparseCore 0:
  19.5 34.1 reduce-scatter.2
  96.1 23.0 reduce-scatter.4
where the time goes:
time: 147 us
  waiting for transfers between devices  56.2 us (38%)
  blocking collectives  33.3 us (23%)
  matrix products  19.9 us (14%)
  other arithmetic  16.7 us (11%)
  between operations  13.7 us (9%)
  starting transfers between devices  3.93 us (3%)
  local copies, waits for them, and re-layouts  3.28 us (2%)
    reduce_scatter x1, waiting for transfers between devices, shards(): lax.psum_scatter(jnp.concatenate([jnp.dot(synthetic, basis_rows, preferre...  31.5 us
    reduce_scatter x1, waiting for transfers between devices, shards(): lax.psum_scatter(running.astype(jnp.bfloat16), ('sub', 'pair'), scatter_d...  23.2 us
    all_gather x1, blocking collectives, shards(): lax.all_gather(adjoint_spec, 'blk', axis=0, tiled=True)  18 us
    dot_general x4, matrix products, pair_tile(): jnp.dot(coupling, column_model, preferred_element_type=jnp.float32)  9.86 us
    another operation x3, other arithmetic  9.36 us
    all_gather x1, blocking collectives, shards(): lax.all_gather(model_spec, ('sub', 'pair'), axis=0, tiled=True)  7.88 us
    all_gather x1, blocking collectives, shards(): lax.all_gather(data_spec, ('sub', 'pair'), axis=0, tiled=True)  7.43 us
    dot_general x3, matrix products, pair_tile(): lax.dot_general(block_data, column_data, contract_last, preferred_element...  4.38 us
  transfers between devices with their start and end apart: 5, of which 4 were waited for; matrix products, arithmetic and copies ran while one was open for 11% of the time, Pallas kernels for 0%

commit v1 on v0

--- a/solution.py
+++ b/solution.py
@@ -1,8 +1,11 @@
+import functools
 import math
 
 import jax
 import jax.numpy as jnp
 from jax import lax
+from jax.experimental import pallas as pl
+from jax.experimental.pallas import tpu as pltpu
 from jax.sharding import PartitionSpec as P
 
 NT = 4096
@@ -134,6 +137,325 @@
     ).astype(jnp.bfloat16)
 
 
+MESH = pl.DeviceIdType.MESH
+RC = 32
+FINE = 32
+TILE = 256
+
+
+def trig(samples, shape):
+    bins = F_LO + lax.broadcasted_iota(jnp.int32, shape, 1)
+    angle = ((samples * bins) % NT).astype(jnp.float32) * (2.0 * math.pi / NT)
+    return jnp.cos(angle), jnp.sin(angle)
+
+
+def fused_kernel(
+    steps_z, factor, syn, obs, weights, mask, out,
+    basis, tab, part, go_up, go_down, from_low, from_high, spec, own_rows, rates,
+    power_col, power_row, gain, acc,
+    send_z, recv_z, send_x, send_c, send_relay, recv_g,
+):
+    f32, bf16 = jnp.float32, jnp.bfloat16
+    event, z = lax.axis_index("events"), lax.axis_index("blk")
+    sub, core = lax.axis_index("sub"), lax.axis_index("pair")
+    last = steps_z - 1
+    rows, span = syn.shape
+    stations = weights.shape[1]
+    pieces = mask.shape[0]
+    chunks = rows // RC
+    me, across = sub * 2 + core, (1 - sub) * 2 + core
+    twin, diagonal = sub * 2 + 1 - core, (1 - sub) * 2 + 1 - core
+    up, down = (event, z + 1, sub, core), (event, z - 1, sub, core)
+    over, beside = (event, z, 1 - sub, core), (event, z, sub, 1 - core)
+
+    barrier = pltpu.get_barrier_semaphore()
+    for device in (over, beside):
+        pl.semaphore_signal(barrier, inc=1, device_id=device, device_id_type=MESH)
+
+    @pl.when(z > 0)
+    def _():
+        pl.semaphore_signal(barrier, inc=1, device_id=down, device_id_type=MESH)
+
+    @pl.when(z < last)
+    def _():
+        pl.semaphore_signal(barrier, inc=1, device_id=up, device_id_type=MESH)
+
+    coarse = span // FINE
+    shape = (coarse, NF)
+    coarse_cos, coarse_sin = trig(
+        z * span + FINE * lax.broadcasted_iota(jnp.int32, shape, 0), shape
+    )
+    tab[0] = coarse_cos
+    tab[1] = coarse_sin
+    shape = (FINE, NF)
+    fine_cos, fine_sin = trig(lax.broadcasted_iota(jnp.int32, shape, 0), shape)
+
+    def fill(a, carry):
+        c = tab[0, pl.ds(a, 1), :]
+        s = tab[1, pl.ds(a, 1), :]
+        at = pl.ds(pl.multiple_of(a * FINE, FINE), FINE)
+        basis[at, :NF] = (c * fine_cos - s * fine_sin).astype(bf16)
+        basis[at, NF:] = (-(s * fine_cos + c * fine_sin)).astype(bf16)
+        return carry
+
+    lax.fori_loop(0, coarse, fill, 0)
+
+    scale = 1.0 / math.sqrt(NT)
+
+    def project(j, carry):
+        at = pl.ds(pl.multiple_of(j * TILE, TILE), TILE)
+        columns = basis[:, at]
+        for k, traces in enumerate((syn, obs)):
+            value = jnp.dot(traces[...], columns, preferred_element_type=f32) * scale
+            part[:, k * RC : (k + 1) * RC, at] = value.astype(bf16).reshape(chunks, RC, TILE)
+        return carry
+
+    lax.fori_loop(0, 2 * NF // TILE, project, 0)
+
+    peers = 2 + jnp.where(z > 0, 1, 0) + jnp.where(z < last, 1, 0)
+    pl.semaphore_wait(barrier, peers)
+
+    def remote(source, target, send, recv, device):
+        return pltpu.make_async_remote_copy(
+            src_ref=source, dst_ref=target, send_sem=send, recv_sem=recv,
+            device_id=device, device_id_type=MESH,
+        )
+
+    def upward(source, n):
+        return remote(source.at[n], from_low.at[n], send_z.at[0, n], recv_z.at[0, n], up)
+
+    def downward(source, n):
+        return remote(source.at[n], from_high.at[n], send_z.at[1, n], recv_z.at[1, n], down)
+
+    def to_over(n):
+        return remote(spec.at[me, n], spec.at[me, n], send_x.at[n], recv_g.at[me, n], over)
+
+    def to_beside(n):
+        return remote(spec.at[me, n], spec.at[me, n], send_c.at[n], recv_g.at[me, n], beside)
+
+    def relay(n):
+        return remote(
+            spec.at[across, n], spec.at[across, n], send_relay.at[n], recv_g.at[across, n], beside
+        )
+
+    def arrived(member, n):
+        remote(spec.at[member, n], spec.at[member, n], send_x.at[n], recv_g.at[member, n], over).wait_recv()
+
+    @pl.when(z == 0)
+    def _():
+        lax.fori_loop(0, chunks, lambda n, c: (upward(part, n).start(), c)[1], 0)
+        from_low[...] = jnp.zeros_like(from_low)
+
+    @pl.when(z == last)
+    def _():
+        lax.fori_loop(0, chunks, lambda n, c: (downward(part, n).start(), c)[1], 0)
+        from_high[...] = jnp.zeros_like(from_high)
+
+    span_piece = stations // pieces
+    own_station = me * rows + lax.broadcasted_iota(jnp.int32, (rows, pieces), 0)
+    behind = own_station - span_piece * lax.broadcasted_iota(jnp.int32, (rows, pieces), 1)
+    own_piece = jnp.where((behind >= 0) & (behind < span_piece), 1.0, 0.0).astype(bf16)
+    links = mask[...].astype(f32).astype(bf16)
+    link_there = jnp.dot(own_piece, links, preferred_element_type=f32).astype(bf16)
+    link_back = lax.dot_general(
+        own_piece, links, (((1,), (1,)), ((), ())), preferred_element_type=f32
+    ).astype(bf16)
+    station = lax.broadcasted_iota(jnp.int32, (pieces, stations), 1)
+    behind = station - span_piece * lax.broadcasted_iota(jnp.int32, (pieces, stations), 0)
+    every_piece = jnp.where((behind >= 0) & (behind < span_piece), 1.0, 0.0).astype(bf16)
+    gain_row = weights[...].astype(f32)
+    column = lax.broadcasted_iota(jnp.int32, (rows, stations), 1)
+    row = me * rows + lax.broadcasted_iota(jnp.int32, (rows, stations), 0)
+    gain_col = jnp.sum(jnp.where(column == row, gain_row, 0.0), axis=1, keepdims=True)
+    gain[...] = (factor * gain_col) * gain_row * jnp.maximum(
+        jnp.dot(link_there, every_piece, preferred_element_type=f32),
+        jnp.dot(link_back, every_piece, preferred_element_type=f32),
+    )
+
+    angular = 2.0 * math.pi / NT * (
+        F_LO + lax.broadcasted_iota(jnp.int32, (1, NF), 1)
+    ).astype(f32)
+
+    def take(member, n):
+        at = pl.ds(pl.multiple_of(member * rows + n * RC, RC), RC)
+        value = spec[member, n].astype(f32)
+        model_lo = (-angular * value[:RC, NF:]).astype(bf16)
+        model_hi = (angular * value[:RC, :NF]).astype(bf16)
+        rates[at, :NF] = model_lo
+        rates[at, NF : 2 * NF] = model_hi
+        rates[at, 2 * NF : 3 * NF] = (angular * value[RC:, NF:]).astype(bf16)
+        rates[at, 3 * NF :] = (-angular * value[RC:, :NF]).astype(bf16)
+        square = jnp.square(model_lo.astype(f32)) + jnp.square(model_hi.astype(f32))
+        power_col[at, :] = jnp.broadcast_to(
+            jnp.sum(square, axis=1, keepdims=True), (RC, 128)
+        )
+
+    def within(n):
+        return (n >= 0) & (n < chunks)
+
+    far = jnp.maximum(z, last - z)
+
+    def step(s, carry):
+        n_low, n_high, n_own = s - z, s - (last - z), s - far
+
+        @pl.when(within(n_low) & (z > 0))
+        def _():
+            upward(part, n_low).wait_recv()
+
+            @pl.when(z < last)
+            def _():
+                go_up[n_low] = (part[n_low].astype(f32) + from_low[n_low].astype(f32)).astype(bf16)
+                upward(go_up, n_low).start()
+
+        @pl.when(within(n_high) & (z < last))
+        def _():
+            downward(part, n_high).wait_recv()
+
+            @pl.when(z > 0)
+            def _():
+                go_down[n_high] = (
+                    part[n_high].astype(f32) + from_high[n_high].astype(f32)
+                ).astype(bf16)
+                downward(go_down, n_high).start()
+
+        @pl.when(within(n_own))
+        def _():
+            spec[me, n_own] = (
+                part[n_own].astype(f32)
+                + from_low[n_own].astype(f32)
+                + from_high[n_own].astype(f32)
+            ).astype(bf16)
+            to_over(n_own).start()
+            to_beside(n_own).start()
+            at = pl.ds(pl.multiple_of(n_own * RC, RC), RC)
+            own_rows[at, : 2 * NF] = spec[me, n_own, :RC, :]
+            own_rows[at, 2 * NF :] = spec[me, n_own, RC:, :]
+            take(me, n_own)
+
+        @pl.when(within(n_own - 2))
+        def _():
+            n = n_own - 2
+            arrived(across, n)
+            relay(n).start()
+            arrived(twin, n)
+            take(across, n)
+            take(twin, n)
+
+        @pl.when(within(n_own - 3))
+        def _():
+            n = n_own - 3
+            arrived(diagonal, n)
+            take(diagonal, n)
+
+        return carry
+
+    lax.fori_loop(0, chunks + last + 3, step, 0)
+
+    eye = lax.broadcasted_iota(jnp.int32, (128, 128), 0) == lax.broadcasted_iota(
+        jnp.int32, (128, 128), 1
+    )
+
+    def turn(q, carry):
+        at = pl.ds(pl.multiple_of(q * 128, 128), 128)
+        power_row[:, at] = jnp.sum(
+            jnp.where(eye, power_col[at, :], 0.0), axis=0, keepdims=True
+        )
+        return carry
+
+    lax.fori_loop(0, stations // 128, turn, 0)
+    own_power = power_col[pl.ds(pl.multiple_of(me * rows, RC), rows), :][:, :1]
+    acc[...] = jnp.zeros_like(acc)
+
+    def pair_tile(q, carry):
+        at = pl.ds(pl.multiple_of(q * TILE, TILE), TILE)
+        cross = lax.dot_general(
+            own_rows[...], rates[at, :], (((1,), (1,)), ((), ())), preferred_element_type=f32
+        )
+        normalizer = 0.5 * (own_power + power_row[:, at]) + epsilon
+        coupling = (gain[:, at] * cross / normalizer).astype(bf16)
+        acc[...] += jnp.dot(coupling, rates[at, : 2 * NF], preferred_element_type=f32)
+        return carry
+
+    lax.fori_loop(0, stations // TILE, pair_tile, 0)
+    own_rows[:, : 2 * NF] = acc[...].astype(bf16)
+    inverse_scale = 1.0 / math.sqrt(NF)
+
+    def to_time(j, carry):
+        at = pl.ds(pl.multiple_of(j * TILE, TILE), TILE)
+        out[:, at] = (
+            lax.dot_general(
+                own_rows[:, : 2 * NF], basis[at, :], (((1,), (1,)), ((), ())),
+                preferred_element_type=f32,
+            )
+            * inverse_scale
+        ).astype(bf16)
+        return carry
+
+    lax.fori_loop(0, span // TILE, to_time, 0)
+
+    def drain(n, carry):
+        @pl.when(z < last)
+        def _():
+            upward(part, n).wait_send()
+
+        @pl.when(z > 0)
+        def _():
+            downward(part, n).wait_send()
+
+        to_over(n).wait_send()
+        to_beside(n).wait_send()
+        relay(n).wait_send()
+        return carry
+
+    lax.fori_loop(0, chunks, drain, 0)
+
+
+def fused_shards(synthetic, observed, station_weights, pair_mask):
+    rows, span = synthetic.shape
+    stations = station_weights.shape[0]
+    members = stations // rows
+    chunks = rows // RC
+    bf16, f32 = jnp.bfloat16, jnp.float32
+    slab = pltpu.VMEM((chunks, 2 * RC, 2 * NF), bf16)
+    vmem = pl.BlockSpec(memory_space=pltpu.VMEM)
+    return pl.pallas_call(
+        functools.partial(fused_kernel, lax.axis_size("blk"), 4.0 / math.sqrt(stations)),
+        out_shape=jax.ShapeDtypeStruct((rows, span), bf16),
+        in_specs=[vmem] * 4,
+        out_specs=vmem,
+        scratch_shapes=[
+            pltpu.VMEM((span, 2 * NF), bf16),
+            pltpu.VMEM((2, span // FINE, NF), f32),
+            slab, slab, slab, slab, slab,
+            pltpu.VMEM((members, chunks, 2 * RC, 2 * NF), bf16),
+            pltpu.VMEM((rows, 4 * NF), bf16),
+            pltpu.VMEM((stations, 4 * NF), bf16),
+            pltpu.VMEM((stations, 128), f32),
+            pltpu.VMEM((1, stations), f32),
+            pltpu.VMEM((rows, stations), f32),
+            pltpu.VMEM((rows, 2 * NF), f32),
+            pltpu.SemaphoreType.DMA((2, chunks)),
+            pltpu.SemaphoreType.DMA((2, chunks)),
+            pltpu.SemaphoreType.DMA((chunks,)),
+            pltpu.SemaphoreType.DMA((chunks,)),
+            pltpu.SemaphoreType.DMA((chunks,)),
+            pltpu.SemaphoreType.DMA((members, chunks)),
+        ],
+        compiler_params=pltpu.CompilerParams(
+            collective_id=0, has_side_effects=True, vmem_limit_bytes=60 * 2**20
+        ),
+    )(synthetic, observed, station_weights.reshape(1, stations), pair_mask)
+
+
+def dispatch(mesh, *arrays):
+    rows, span = arrays[0].shape
+    stations = arrays[2].shape[0]
+    fits = 28 * NF * stations + 40 * NF * rows + 4 * rows * stations < 44 * 2**20
+    whole = rows % RC == 0 and span % TILE == 0 and stations % TILE == 0
+    plane = mesh.shape["sub"] == 2 and mesh.shape["pair"] == 2 and mesh.shape["blk"] > 1
+    return (fused_shards if fits and whole and plane else shards)(*arrays)
+
+
 def solution(mesh):
     placed = (
         P(("events", "sub", "pair"), "blk"),
@@ -142,7 +464,7 @@
         P("events", None),
     )
     return jax.shard_map(
-        shards,
+        functools.partial(dispatch, mesh),
         mesh=mesh,
         in_specs=placed,
         out_specs=P(("events", "sub", "pair"), "blk"),

time: 147 us -> 70.5 us (0.48)
  Pallas kernels: 0 us -> 66.4 us
  waiting for transfers between devices: 56.2 us -> 0 us
  blocking collectives: 33.3 us -> 0 us
  matrix products: 19.9 us -> 0 us
  other arithmetic: 16.7 us -> 0 us
  between operations: 13.7 us -> 0.01 us
  starting transfers between devices: 3.93 us -> 0 us
    pallas_call x0 -> x1, Pallas kernels: none -> 66.4 us  [fused_shards(): pl.pallas_call(functools.partial(fused_kernel, lax.axis_size('blk'), 4.0...]
    reduce_scatter x2 -> x0, waiting for transfers between devices: 54.7 us -> none  [the longest x1 31.5 us: shards(): lax.psum_scatter(jnp.concatenate([jnp.dot(synthetic, basis_rows, preferre...]
    all_gather x3 -> x0, blocking collectives: 33.3 us -> none  [the longest x1 18 us: shards(): lax.all_gather(adjoint_spec, 'blk', axis=0, tiled=True)]
    dot_general x11 -> x0, matrix products: 19.9 us -> none  [the longest x4 9.86 us: pair_tile(): jnp.dot(coupling, column_model, preferred_element_type=jnp.float32)]
    another operation x3 -> x0, other arithmetic: 9.36 us -> none
    reduce_sum x5 -> x0, other arithmetic: 4.09 us -> none  [the longest x4 3.87 us: pair_tile(): column_power = jnp.sum(jnp.square(column_model.astype(jnp.float32)), axis=1)]
    ppermute x3 -> x0, starting transfers between devices: 3.88 us -> none  [from_behind(): return lax.ppermute(value, axis, pairs)]
    concatenate x2 -> x0, other arithmetic: 1.93 us -> none  [the longest x1 1.18 us: shards(): jnp.concatenate([jnp.dot(synthetic, basis_rows, preferred_element_type=jn...]
  transfers between devices with their start and end apart: 5 -> 0, of which waited for: 4 -> 0; matrix products, arithmetic and copies ran while one was open for 11% -> 0% of each run, Pallas kernels for 0% -> 0%
where the time goes in v1:
time: 70.5 us; the launch traced here: 69.7 us
  Pallas kernels  66.4 us (94%)
  local copies, waits for them, and re-layouts  3.26 us (5%)
    pallas_call x1, Pallas kernels, fused_shards(): pl.pallas_call(functools.partial(fused_kernel, lax.axis_size('blk'), 4.0...  66.4 us
    unnamed x1, local copies, waits for them, and re-layouts  1.97 us

profile of v1, /device:TPU:0, one launch (start us, length us, event | category | flops | bytes accessed | tf_op | source)
XLA Modules:
  0.0 69.7 jit_solution(6930496462651958359)
XLA Ops:
  0.0 1.3 %reshape.3.weights = s32[1,1280]{1,0:T(1,128)} reshape(s32[1280]{0:T(1024)} %param.6) | data formatting | bytes 10240 | tf_op jit(solution)/shard_map/reshape | solution.py:447
  1.3 66.4 %shard_map.46 = bf16[320,1024]{1,0:T(8,128)(2,1)} custom-call(bf16[320,1024]{1,0:T(8,128)(2,1)} %syn.1, bf16[320,1024]{1,0:T(8,128)(2,1)} %obs.1, s32[1,1280]{1,0:T(1,128)} %reshape.3.weights, s32[16,16]{1,0:T(8,128)} %mask.1), custom_call_target="tpu_custom_call" | custom-call | tf_op jit(solution)/shard_map/pallas_call | solution.py:421
  67.7 2.0 %copy.6 = bf16[320,1024]{1,0:T(8,128)(2,1)} copy(bf16[320,1024]{1,0:T(8,128)(2,1)} %shard_map.46) | data formatting | bytes 1310720

commit v2 on v1

--- a/solution.py
+++ b/solution.py
@@ -138,9 +138,14 @@
 
 
 MESH = pl.DeviceIdType.MESH
-RC = 32
+RC = 16
+SKEW = 3
+OVER = 3
+BESIDE = 5
 FINE = 32
 TILE = 256
+MEMBERS = 4
+BATCH = TILE // MEMBERS
 
 
 def trig(samples, shape):
@@ -152,7 +157,7 @@
 def fused_kernel(
     steps_z, factor, syn, obs, weights, mask, out,
     basis, tab, part, go_up, go_down, from_low, from_high, spec, own_rows, rates,
-    power_col, power_row, gain, acc,
+    power_col, own_power, gain, acc,
     send_z, recv_z, send_x, send_c, send_relay, recv_g,
 ):
     f32, bf16 = jnp.float32, jnp.bfloat16
@@ -160,7 +165,7 @@
     sub, core = lax.axis_index("sub"), lax.axis_index("pair")
     last = steps_z - 1
     rows, span = syn.shape
-    stations = weights.shape[1]
+    stations = weights.shape[0] * 128
     pieces = mask.shape[0]
     chunks = rows // RC
     me, across = sub * 2 + core, (1 - sub) * 2 + core
@@ -250,6 +255,9 @@
     def _():
         lax.fori_loop(0, chunks, lambda n, c: (downward(part, n).start(), c)[1], 0)
         from_high[...] = jnp.zeros_like(from_high)
+
+    def station_of(place):
+        return (place % TILE) // BATCH * rows + place // TILE * BATCH + place % BATCH
 
     span_piece = stations // pieces
     own_station = me * rows + lax.broadcasted_iota(jnp.int32, (rows, pieces), 0)
@@ -260,11 +268,18 @@
     link_back = lax.dot_general(
         own_piece, links, (((1,), (1,)), ((), ())), preferred_element_type=f32
     ).astype(bf16)
-    station = lax.broadcasted_iota(jnp.int32, (pieces, stations), 1)
+    station = station_of(lax.broadcasted_iota(jnp.int32, (pieces, stations), 1))
     behind = station - span_piece * lax.broadcasted_iota(jnp.int32, (pieces, stations), 0)
     every_piece = jnp.where((behind >= 0) & (behind < span_piece), 1.0, 0.0).astype(bf16)
-    gain_row = weights[...].astype(f32)
-    column = lax.broadcasted_iota(jnp.int32, (rows, stations), 1)
+    starts = [m * rows + b * BATCH for b in range(rows // BATCH) for m in range(MEMBERS)]
+    gain_row = jnp.concatenate(
+        [
+            weights[t // 128 : t // 128 + 1, t % 128 : t % 128 + BATCH].astype(f32)
+            for t in starts
+        ],
+        axis=1,
+    )
+    column = station_of(lax.broadcasted_iota(jnp.int32, (rows, stations), 1))
     row = me * rows + lax.broadcasted_iota(jnp.int32, (rows, stations), 0)
     gain_col = jnp.sum(jnp.where(column == row, gain_row, 0.0), axis=1, keepdims=True)
     gain[...] = (factor * gain_col) * gain_row * jnp.maximum(
@@ -276,8 +291,11 @@
         F_LO + lax.broadcasted_iota(jnp.int32, (1, NF), 1)
     ).astype(f32)
 
+    def place_of(member, n):
+        return n * RC // BATCH * TILE + member * BATCH + n * RC % BATCH
+
     def take(member, n):
-        at = pl.ds(pl.multiple_of(member * rows + n * RC, RC), RC)
+        at = pl.ds(pl.multiple_of(place_of(member, n), RC), RC)
         value = spec[member, n].astype(f32)
         model_lo = (-angular * value[:RC, NF:]).astype(bf16)
         model_hi = (angular * value[:RC, :NF]).astype(bf16)
@@ -290,13 +308,45 @@
             jnp.sum(square, axis=1, keepdims=True), (RC, 128)
         )
 
+    eye = lax.broadcasted_iota(jnp.int32, (128, 128), 0) == lax.broadcasted_iota(
+        jnp.int32, (128, 128), 1
+    )
+
+    def pair_tile(q):
+        at = pl.ds(pl.multiple_of(q * TILE, TILE), TILE)
+        power_row = jnp.concatenate(
+            [
+                jnp.sum(
+                    jnp.where(
+                        eye, power_col[pl.ds(pl.multiple_of(q * TILE + k, 128), 128), :], 0.0
+                    ),
+                    axis=0,
+                    keepdims=True,
+                )
+                for k in range(0, TILE, 128)
+            ],
+            axis=1,
+        )
+        cross = lax.dot_general(
+            own_rows[...], rates[at, :], (((1,), (1,)), ((), ())), preferred_element_type=f32
+        )
+        normalizer = 0.5 * (own_power[:, :1] + power_row) + epsilon
+        coupling = (gain[:, at] * cross / normalizer).astype(bf16)
+        acc[...] += jnp.dot(coupling, rates[at, : 2 * NF], preferred_element_type=f32)
+
     def within(n):
         return (n >= 0) & (n < chunks)
 
+    acc[...] = jnp.zeros_like(acc)
     far = jnp.maximum(z, last - z)
 
+    tiles = stations // TILE
+    first_tile = max(
+        [chunks] + [(q + 1) * (BATCH // RC) - 1 + BESIDE - q for q in range(tiles - 1)]
+    )
+
     def step(s, carry):
-        n_low, n_high, n_own = s - z, s - (last - z), s - far
+        n_low, n_high, n_own = s - SKEW * z, s - SKEW * (last - z), s - SKEW * far
 
         @pl.when(within(n_low) & (z > 0))
         def _():
@@ -331,52 +381,32 @@
             own_rows[at, : 2 * NF] = spec[me, n_own, :RC, :]
             own_rows[at, 2 * NF :] = spec[me, n_own, RC:, :]
             take(me, n_own)
-
-        @pl.when(within(n_own - 2))
-        def _():
-            n = n_own - 2
+            own_power[at, :] = power_col[pl.ds(pl.multiple_of(place_of(me, n_own), RC), RC), :]
+
+        @pl.when(within(n_own - OVER))
+        def _():
+            n = n_own - OVER
             arrived(across, n)
             relay(n).start()
             arrived(twin, n)
             take(across, n)
             take(twin, n)
 
-        @pl.when(within(n_own - 3))
-        def _():
-            n = n_own - 3
+        @pl.when(within(n_own - BESIDE))
+        def _():
+            n = n_own - BESIDE
             arrived(diagonal, n)
             take(diagonal, n)
 
+        @pl.when((n_own >= first_tile) & (n_own < first_tile + tiles - 1))
+        def _():
+            pair_tile(n_own - first_tile)
+
         return carry
 
-    lax.fori_loop(0, chunks + last + 3, step, 0)
-
-    eye = lax.broadcasted_iota(jnp.int32, (128, 128), 0) == lax.broadcasted_iota(
-        jnp.int32, (128, 128), 1
-    )
-
-    def turn(q, carry):
-        at = pl.ds(pl.multiple_of(q * 128, 128), 128)
-        power_row[:, at] = jnp.sum(
-            jnp.where(eye, power_col[at, :], 0.0), axis=0, keepdims=True
-        )
-        return carry
-
-    lax.fori_loop(0, stations // 128, turn, 0)
-    own_power = power_col[pl.ds(pl.multiple_of(me * rows, RC), rows), :][:, :1]
-    acc[...] = jnp.zeros_like(acc)
-
-    def pair_tile(q, carry):
-        at = pl.ds(pl.multiple_of(q * TILE, TILE), TILE)
-        cross = lax.dot_general(
-            own_rows[...], rates[at, :], (((1,), (1,)), ((), ())), preferred_element_type=f32
-        )
-        normalizer = 0.5 * (own_power + power_row[:, at]) + epsilon
-        coupling = (gain[:, at] * cross / normalizer).astype(bf16)
-        acc[...] += jnp.dot(coupling, rates[at, : 2 * NF], preferred_element_type=f32)
-        return carry
-
-    lax.fori_loop(0, stations // TILE, pair_tile, 0)
+    lax.fori_loop(0, max(chunks + BESIDE, first_tile + tiles - 1) + SKEW * last, step, 0)
+
+    pair_tile(stations // TILE - 1)
     own_rows[:, : 2 * NF] = acc[...].astype(bf16)
     inverse_scale = 1.0 / math.sqrt(NF)
 
@@ -416,6 +446,7 @@
     members = stations // rows
     chunks = rows // RC
     bf16, f32 = jnp.bfloat16, jnp.float32
+    weights = station_weights.reshape(stations // 128, 128)
     slab = pltpu.VMEM((chunks, 2 * RC, 2 * NF), bf16)
     vmem = pl.BlockSpec(memory_space=pltpu.VMEM)
     return pl.pallas_call(
@@ -431,7 +462,7 @@
             pltpu.VMEM((rows, 4 * NF), bf16),
             pltpu.VMEM((stations, 4 * NF), bf16),
             pltpu.VMEM((stations, 128), f32),
-            pltpu.VMEM((1, stations), f32),
+            pltpu.VMEM((rows, 128), f32),
             pltpu.VMEM((rows, stations), f32),
             pltpu.VMEM((rows, 2 * NF), f32),
             pltpu.SemaphoreType.DMA((2, chunks)),
@@ -442,16 +473,16 @@
             pltpu.SemaphoreType.DMA((members, chunks)),
         ],
         compiler_params=pltpu.CompilerParams(
-            collective_id=0, has_side_effects=True, vmem_limit_bytes=60 * 2**20
+            collective_id=0, has_side_effects=True, vmem_limit_bytes=40 * 2**20
         ),
-    )(synthetic, observed, station_weights.reshape(1, stations), pair_mask)
+    )(synthetic, observed, weights, pair_mask)
 
 
 def dispatch(mesh, *arrays):
     rows, span = arrays[0].shape
     stations = arrays[2].shape[0]
     fits = 28 * NF * stations + 40 * NF * rows + 4 * rows * stations < 44 * 2**20
-    whole = rows % RC == 0 and span % TILE == 0 and stations % TILE == 0
+    whole = rows % BATCH == 0 and span % TILE == 0 and stations % TILE == 0
     plane = mesh.shape["sub"] == 2 and mesh.shape["pair"] == 2 and mesh.shape["blk"] > 1
     return (fused_shards if fits and whole and plane else shards)(*arrays)
 

time: 70.5 us -> 60.5 us (0.86)
  Pallas kernels: 66.4 us -> 55.8 us
  local copies, waits for them, and re-layouts: 3.26 us -> 4.41 us
    pallas_call x1, Pallas kernels: 66.4 us -> 55.8 us  [fused_shards(): pl.pallas_call(functools.partial(fused_kernel, lax.axis_size('blk'), 4.0...]
    unnamed x1 -> x9, local copies, waits for them, and re-layouts: 1.97 us -> 4.41 us
    reshape x1 -> x0, local copies, waits for them, and re-layouts: 1.29 us -> none  [fused_shards(): station_weights.reshape(1, stations)]
where the time goes in v2:
time: 60.5 us; the launch traced here: 60.2 us
  Pallas kernels  55.8 us (92%)
  local copies, waits for them, and re-layouts  4.41 us (7%)
    pallas_call x1, Pallas kernels, fused_shards(): pl.pallas_call(functools.partial(fused_kernel, lax.axis_size('blk'), 4.0...  55.8 us
    unnamed x9, local copies, waits for them, and re-layouts  4.41 us

profile of v2, /device:TPU:0, one launch (start us, length us, event | category | flops | bytes accessed | tf_op | source)
XLA Modules:
  0.0 60.2 jit_solution(7291977907317091953)
XLA Ops:
  0.0 0.0 copy-start
  0.0 1.1 %copy-done = bf16[320,1024]{1,0:T(8,128)(2,1)S(1)} copy-done((bf16[320,1024]{1,0:T(8,128)(2,1)S(1)}, bf16[320,1024]{1,0:T(8,128)(2,1)}, u32[]{:S(2)}) %copy-start) | copy-done | bytes 655384
  1.1 0.0 copy-start.1
  1.1 1.1 %copy-done.1 = bf16[320,1024]{1,0:T(8,128)(2,1)S(1)} copy-done((bf16[320,1024]{1,0:T(8,128)(2,1)S(1)}, bf16[320,1024]{1,0:T(8,128)(2,1)}, u32[]{:S(2)}) %copy-start.1) | copy-done | bytes 655384
  2.2 0.0 copy-start.2
  2.2 0.7 %copy-done.2 = s32[1280]{0:T(1024)S(1)} copy-done((s32[1280]{0:T(1024)S(1)}, s32[1280]{0:T(1024)}, u32[]{:S(2)}) %copy-start.2) | copy-done | bytes 5144
  2.9 0.0 copy-start.3
  2.9 0.7 %copy-done.3 = s32[16,16]{1,0:T(8,128)S(1)} copy-done((s32[16,16]{1,0:T(8,128)S(1)}, s32[16,16]{1,0:T(8,128)}, u32[]{:S(2)}) %copy-start.3) | copy-done | bytes 1048
  3.6 55.8 %shard_map.46 = bf16[320,1024]{1,0:T(8,128)(2,1)S(1)} custom-call(bf16[320,1024]{1,0:T(8,128)(2,1)S(1)} %copy-done, bf16[320,1024]{1,0:T(8,128)(2,1)S(1)} %copy-done.1, s32[10,128]{1,0:T(8,128)S(1)} %bitcast.1, s32[16,16]{1,0:T(8,128)S(1)} %copy-done.3), custom_call_target="tpu_custom_call" | custom-call | tf_op jit(solution)/shard_map/pallas_call | solution.py:452
  59.4 0.8 %copy.6 = bf16[320,1024]{1,0:T(8,128)(2,1)} copy(bf16[320,1024]{1,0:T(8,128)(2,1)S(1)} %shard_map.46) | data formatting | bytes 1310720
Async XLA Ops:
  0.0 1.1 %copy-start = (bf16[320,1024]{1,0:T(8,128)(2,1)S(1)}, bf16[320,1024]{1,0:T(8,128)(2,1)}, u32[]{:S(2)}) copy-start(bf16[320,1024]{1,0:T(8,128)(2,1)} %syn.1) | copy-start | bytes 1966084
  1.1 1.1 %copy-start.1 = (bf16[320,1024]{1,0:T(8,128)(2,1)S(1)}, bf16[320,1024]{1,0:T(8,128)(2,1)}, u32[]{:S(2)}) copy-start(bf16[320,1024]{1,0:T(8,128)(2,1)} %obs.1) | copy-start | bytes 1966084
  2.2 0.7 %copy-start.2 = (s32[1280]{0:T(1024)S(1)}, s32[1280]{0:T(1024)}, u32[]{:S(2)}) copy-start(s32[1280]{0:T(1024)} %param.6) | copy-start | bytes 15364
  2.9 0.7 %copy-start.3 = (s32[16,16]{1,0:T(8,128)S(1)}, s32[16,16]{1,0:T(8,128)}, u32[]{:S(2)}) copy-start(s32[16,16]{1,0:T(8,128)} %mask.1) | copy-start | bytes 3076

commit v3 on v2

--- a/solution.py
+++ b/solution.py
@@ -155,10 +155,11 @@
 
 
 def fused_kernel(
-    steps_z, factor, syn, obs, weights, mask, out,
+    steps_z, factor, syn_hbm, obs_hbm, weights_hbm, mask_hbm, out,
+    syn, obs, weights, mask,
     basis, tab, part, go_up, go_down, from_low, from_high, spec, own_rows, rates,
     power_col, own_power, gain, acc,
-    send_z, recv_z, send_x, send_c, send_relay, recv_g,
+    send_z, recv_z, send_x, send_c, send_relay, recv_g, load,
 ):
     f32, bf16 = jnp.float32, jnp.bfloat16
     event, z = lax.axis_index("events"), lax.axis_index("blk")
@@ -173,6 +174,15 @@
     up, down = (event, z + 1, sub, core), (event, z - 1, sub, core)
     over, beside = (event, z, 1 - sub, core), (event, z, sub, 1 - core)
 
+    loads = [
+        pltpu.make_async_copy(source, target, load.at[k])
+        for k, (source, target) in enumerate(
+            ((syn_hbm, syn), (obs_hbm, obs), (weights_hbm, weights), (mask_hbm, mask))
+        )
+    ]
+    for copy in loads:
+        copy.start()
+
     barrier = pltpu.get_barrier_semaphore()
     for device in (over, beside):
         pl.semaphore_signal(barrier, inc=1, device_id=device, device_id_type=MESH)
@@ -207,15 +217,27 @@
 
     scale = 1.0 / math.sqrt(NT)
 
-    def project(j, carry):
-        at = pl.ds(pl.multiple_of(j * TILE, TILE), TILE)
-        columns = basis[:, at]
-        for k, traces in enumerate((syn, obs)):
-            value = jnp.dot(traces[...], columns, preferred_element_type=f32) * scale
-            part[:, k * RC : (k + 1) * RC, at] = value.astype(bf16).reshape(chunks, RC, TILE)
-        return carry
-
-    lax.fori_loop(0, 2 * NF // TILE, project, 0)
+    def project(first, count):
+        def columns_of(j, carry):
+            at = pl.ds(pl.multiple_of(j * TILE, TILE), TILE)
+            columns = basis[:, at]
+            for k, traces in enumerate((syn, obs)):
+                value = scale * jnp.dot(
+                    traces[first * RC : (first + count) * RC, :],
+                    columns,
+                    preferred_element_type=f32,
+                )
+                part[first : first + count, k * RC : (k + 1) * RC, at] = value.astype(
+                    bf16
+                ).reshape(count, RC, TILE)
+            return carry
+
+        lax.fori_loop(0, 2 * NF // TILE, columns_of, 0)
+
+    for copy in loads[:2]:
+        copy.wait()
+    early = BATCH // RC
+    project(0, early)
 
     peers = 2 + jnp.where(z > 0, 1, 0) + jnp.where(z < last, 1, 0)
     pl.semaphore_wait(barrier, peers)
@@ -246,15 +268,29 @@
     def arrived(member, n):
         remote(spec.at[member, n], spec.at[member, n], send_x.at[n], recv_g.at[member, n], over).wait_recv()
 
+    def launch(first, end):
+        @pl.when(z == 0)
+        def _():
+            lax.fori_loop(first, end, lambda n, c: (upward(part, n).start(), c)[1], 0)
+
+        @pl.when(z == last)
+        def _():
+            lax.fori_loop(first, end, lambda n, c: (downward(part, n).start(), c)[1], 0)
+
+    launch(0, early)
+    project(early, chunks - early)
+    launch(early, chunks)
+
     @pl.when(z == 0)
     def _():
-        lax.fori_loop(0, chunks, lambda n, c: (upward(part, n).start(), c)[1], 0)
         from_low[...] = jnp.zeros_like(from_low)
 
     @pl.when(z == last)
     def _():
-        lax.fori_loop(0, chunks, lambda n, c: (downward(part, n).start(), c)[1], 0)
         from_high[...] = jnp.zeros_like(from_high)
+
+    for copy in loads[2:]:
+        copy.wait()
 
     def station_of(place):
         return (place % TILE) // BATCH * rows + place // TILE * BATCH + place % BATCH
@@ -452,9 +488,13 @@
     return pl.pallas_call(
         functools.partial(fused_kernel, lax.axis_size("blk"), 4.0 / math.sqrt(stations)),
         out_shape=jax.ShapeDtypeStruct((rows, span), bf16),
-        in_specs=[vmem] * 4,
+        in_specs=[pl.BlockSpec(memory_space=pltpu.HBM)] * 4,
         out_specs=vmem,
         scratch_shapes=[
+            pltpu.VMEM((rows, span), bf16),
+            pltpu.VMEM((rows, span), bf16),
+            pltpu.VMEM((stations // 128, 128), jnp.int32),
+            pltpu.VMEM(pair_mask.shape, jnp.int32),
             pltpu.VMEM((span, 2 * NF), bf16),
             pltpu.VMEM((2, span // FINE, NF), f32),
             slab, slab, slab, slab, slab,
@@ -471,9 +511,10 @@
             pltpu.SemaphoreType.DMA((chunks,)),
             pltpu.SemaphoreType.DMA((chunks,)),
             pltpu.SemaphoreType.DMA((members, chunks)),
+            pltpu.SemaphoreType.DMA((4,)),
         ],
         compiler_params=pltpu.CompilerParams(
-            collective_id=0, has_side_effects=True, vmem_limit_bytes=40 * 2**20
+            collective_id=0, has_side_effects=True, vmem_limit_bytes=60 * 2**20
         ),
     )(synthetic, observed, weights, pair_mask)
 

time: 60.5 us -> 58 us (0.959)
  local copies, waits for them, and re-layouts: 4.41 us -> 1.97 us
    unnamed x9 -> x1, local copies, waits for them, and re-layouts: 4.41 us -> 1.97 us
where the time goes in v3:
time: 58 us; the launch traced here: 57.8 us
  Pallas kernels  55.9 us (96%)
  local copies, waits for them, and re-layouts  1.97 us (3%)
    pallas_call x1, Pallas kernels, fused_shards(): pl.pallas_call(functools.partial(fused_kernel, lax.axis_size('blk'), 4.0...  55.9 us
    unnamed x1, local copies, waits for them, and re-layouts  1.97 us

profile of v3, /device:TPU:0, one launch (start us, length us, event | category | flops | bytes accessed | tf_op | source)
XLA Modules:
  0.0 57.8 jit_solution(13220528982870078822)
XLA Ops:
  0.0 55.9 %shard_map.46 = bf16[320,1024]{1,0:T(8,128)(2,1)} custom-call(bf16[320,1024]{1,0:T(8,128)(2,1)} %syn_hbm.1, bf16[320,1024]{1,0:T(8,128)(2,1)} %obs_hbm.1, s32[10,128]{1,0:T(8,128)} %bitcast.1, s32[16,16]{1,0:T(8,128)} %mask_hbm.1), custom_call_target="tpu_custom_call" | custom-call | tf_op jit(solution)/shard_map/pallas_call | solution.py:488
  55.9 2.0 %copy.6 = bf16[320,1024]{1,0:T(8,128)(2,1)} copy(bf16[320,1024]{1,0:T(8,128)(2,1)} %shard_map.46) | data formatting | bytes 1310720
